TPU v7x, 1024 devices: a whole 4x8x16 slice. The times are simulated.
1024 devices in a mesh: tok: 128 (over x, y_lo, z), head: 8 (over y_hi, core).
Axes of the slice: x: 4, y: 8 (y_hi: 4, y_lo: 2; y = y_hi * 2 + y_lo), z: 16, core: 2. Of those that a mesh axis runs over, the one named last changes fastest.
Arguments:
- queries_first: bfloat16 [32768, 3072], P('tok', 'head'), may hold values from -180 to 180
- queries_second: bfloat16 [32768, 3072], P('tok', 'head'), may hold values from -180 to 180
- grads_first: bfloat16 [32768, 3072], P('tok', 'head'), may hold values from -6 to 6
- grads_second: bfloat16 [32768, 3072], P('tok', 'head'), may hold values from -6 to 6
- key_states: bfloat16 [32768, 1024], P('tok', 'head'), may hold values from -4.5 to 4.5
- value_states: bfloat16 [32768, 1024], P('tok', 'head'), may hold values from -6 to 6
- doc_lengths: int32 [128], replicated, may hold values from 1 to 768, 32768 in all
- hidden_states: bfloat16 [32768, 3072], P('tok', 'head'), may hold values from -24 to 24
Outputs:
- grad_queries_first: bfloat16 [32768, 3072], P('tok', 'head')
- grad_queries_second: bfloat16 [32768, 3072], P('tok', 'head')
- weight_grad: float32 [3072, 2048], P('tok', 'head')
All inputs are finite; a program needn't handle non-finite values.
Results may differ from a plain program's by a relative error of at most 0.0075.
Values may be sent and summed in bfloat16 or wider, within the bound.
A program may use at most 32 MiB of HBM per device.

v0:
```python
import math

import jax
import jax.numpy as jnp
from jax import lax
from jax.sharding import PartitionSpec as P

HD = 128
REACH = 3


def passed_along(value, axis, steps):
    count = lax.axis_size(axis)
    initial, last = (max(0, -steps), min(count, count - steps))
    return lax.ppermute(value, axis, [(source, source + steps) for source in range(initial, last)])


def document_of(places, doc_ends):
    return jnp.sum((places[:, None] >= doc_ends[None, :]).astype(jnp.int32), axis=1)


def causal_mask(query_places, key_places, doc_ends):
    same_doc = (
        document_of(query_places, doc_ends)[:, None]
        == document_of(jnp.maximum(key_places, 0), doc_ends)[None, :]
    )
    return same_doc & (key_places[None, :] <= query_places[:, None]) & (key_places[None, :] >= 0)


def attend_grads(queries, grad_rows, key_window, value_window, allowed):
    query_rows = queries.shape[0]
    window = key_window.shape[0]
    kv_heads = key_window.shape[1] // HD
    group_size = queries.shape[1] // (kv_heads * HD)
    score_scale = 1.0 / math.sqrt(HD)
    q_four = queries.reshape(query_rows, kv_heads, group_size, HD)
    g_four = grad_rows.reshape(query_rows, kv_heads, group_size, HD)
    k_three = key_window.reshape(window, kv_heads, HD)
    v_three = value_window.reshape(window, kv_heads, HD)
    scores = (
        jnp.einsum("bhgd,whd->hgbw", q_four, k_three, preferred_element_type=jnp.float32)
        * score_scale
    )
    scores = jnp.where(allowed, scores, -1e30)
    row_max = jnp.max(scores, axis=-1, keepdims=True)
    raised = jnp.exp(scores - row_max)
    prob_rows = raised / jnp.sum(raised, axis=-1, keepdims=True)
    prob_half = prob_rows.astype(jnp.bfloat16)
    outputs = jnp.einsum("hgbw,whd->bhgd", prob_half, v_three, preferred_element_type=jnp.float32)
    deltas = jnp.sum(g_four.astype(jnp.float32) * outputs, axis=-1)
    deltas = jnp.transpose(deltas, (1, 2, 0))[..., None]
    grad_prob = jnp.einsum("bhgd,whd->hgbw", g_four, v_three, preferred_element_type=jnp.float32)
    grad_score = (prob_rows * (grad_prob - deltas)).astype(jnp.bfloat16)
    grad_query = (
        jnp.einsum("hgbw,whd->bhgd", grad_score, k_three, preferred_element_type=jnp.float32)
        * score_scale
    ).astype(jnp.bfloat16)
    grad_key = (
        jnp.einsum("hgbw,bhgd->whd", grad_score, q_four, preferred_element_type=jnp.float32)
        * score_scale
    )
    grad_value = jnp.einsum("hgbw,bhgd->whd", prob_half, g_four, preferred_element_type=jnp.float32)
    return (grad_query.reshape(query_rows, -1), grad_key, grad_value)


def projection_term(full_rows, grad_part):
    return lax.dot_general(
        full_rows, grad_part, (((0,), (0,)), ((), ())), preferred_element_type=jnp.float32
    )


def body(
    queries_first,
    queries_second,
    grads_first,
    grads_second,
    key_states,
    value_states,
    doc_lengths,
    hidden_states,
):
    tok_rows = key_states.shape[0]
    kv_width = key_states.shape[1]
    window = (REACH + 1) * tok_rows
    here = lax.axis_index("tok")
    stacked = jnp.concatenate([key_states, value_states], axis=1)
    blocks = [stacked]
    current = stacked
    for hop_count in range(REACH):
        current = passed_along(current, "tok", 1)
        blocks.append(current)
    window_rows = jnp.concatenate(blocks[::-1], axis=0)
    key_window = window_rows[:, :kv_width]
    value_window = window_rows[:, kv_width:]
    doc_ends = jnp.cumsum(doc_lengths)
    query_places = here * tok_rows + jnp.arange(tok_rows, dtype=jnp.int32)
    key_places = (here - REACH) * tok_rows + jnp.arange(window, dtype=jnp.int32)
    allowed = causal_mask(query_places, key_places, doc_ends)
    first_q, first_k, first_v = attend_grads(
        queries_first, grads_first, key_window, value_window, allowed
    )
    second_q, second_k, second_v = attend_grads(
        queries_second, grads_second, key_window, value_window, allowed
    )
    window_grads = jnp.stack([first_k + second_k, first_v + second_v], axis=2).reshape(window, -1)

    def block_term(back_steps):
        return window_grads[(REACH - back_steps) * tok_rows : (REACH - back_steps + 1) * tok_rows]

    running = block_term(0)
    for back_steps in range(1, REACH + 1):
        running = running + passed_along(
            block_term(back_steps).astype(jnp.bfloat16), "tok", -back_steps
        ).astype(jnp.float32)
    kv_grads = running.astype(jnp.bfloat16)
    full_rows = lax.all_gather(hidden_states, "head", axis=1, tiled=True)
    weight_grad = lax.psum_scatter(
        projection_term(full_rows, kv_grads), "tok", scatter_dimension=0, tiled=True
    )
    return (first_q, second_q, weight_grad)


def solution(mesh):
    placed = (
        P("tok", "head"),
        P("tok", "head"),
        P("tok", "head"),
        P("tok", "head"),
        P("tok", "head"),
        P("tok", "head"),
        P(),
        P("tok", "head"),
    )
    return jax.shard_map(
        body,
        mesh=mesh,
        in_specs=placed,
        out_specs=(P("tok", "head"), P("tok", "head"), P("tok", "head")),
        check_vma=False,
    )
```

profile of v0, /device:TPU:16, one launch (start us, length us, event | category | flops | bytes accessed | tf_op | source)
XLA Modules:
  0.0 728.9 jit_solution(17143597557302562338)
XLA Ops:
  7.2 0.0 all-gather.2.cloned.1.call-start
  7.2 0.9 constant_dynamic-update-slice_fusion.1
  8.1 0.9 constant_dynamic-update-slice_fusion
  9.0 4.3 collective-permute-start
  13.3 0.0 reduce-scatter.4.cloned.1.call-start
  13.4 0.8 copy.89
  14.1 0.2 reduce-window.8
  14.3 0.1 reduce.6
  14.4 0.2 convert_reduce_fusion.1
  14.6 1.4 collective-permute-done
  16.0 4.4 collective-permute-start.1
  20.4 1.1 copy.101
  21.5 1.1 copy.103
  22.5 1.1 copy.92
  23.6 1.1 copy.94
  24.7 1.1 copy.90
  25.7 0.1 copy.99
  25.9 0.4 convert_reduce_fusion
  26.3 4.3 collective-permute-start.2
  30.6 0.9 and_and_fusion
  31.5 1.6 collective-permute-done.2
  33.1 0.6 fusion.91
  33.7 1.0 fusion.9
  34.7 1.3 fusion.7
  36.0 1.1 fusion.79
  37.0 1.1 fusion.3
  38.2 0.6 fusion.31
  38.8 1.1 fusion.82
  39.9 1.1 fusion.1
  41.0 0.6 fusion.46
  41.7 1.1 fusion.28
  42.8 1.1 fusion.52
  43.9 0.1 fusion.85
  44.0 1.3 collective-permute-start.3
  45.3 1.3 collective-permute-start.4
  46.6 1.3 collective-permute-start.5
  47.9 4.4 collective-permute-done.3
  52.3 7.1 collective-permute-done.4
  59.5 6.8 collective-permute-done.5
  66.2 0.1 fusion.89
  66.3 2.0 convolution_bitcast_fusion
  68.3 2.4 copy.135
  70.7 1.4 copy-done.3
  72.1 1.4 fusion.73
  73.5 0.8 copy.113
  74.3 1.4 fusion.76
  75.6 0.8 copy.112
  76.5 645.6 %reduce-scatter.4.cloned.1.call-done = f32[24,256]{1,0:T(8,128)} async-done(((f32[3072,256]{1,0:T(8,128)}), f32[24,256]{1,0:T(8,128)}) %reduce-scatter.4.cloned.1.call-update) | async-done | bytes 24592
  (22 shorter events, 0.2 us)
Async XLA Ops:
  7.2 18.6 %copy-start.5 = (bf16[256,384]{1,0:T(8,128)(2,1)S(1)}, bf16[256,384]{1,0:T(8,128)(2,1)}, u32[]{:S(2)}) copy-start(bf16[256,384]{1,0:T(8,128)(2,1)} %param.9) | copy-start | bytes 589828
  7.2 59.1 %all-gather.2.cloned.1.call-start = ((), (), s32[]{:S(2)}) async-start(), calls=%async_computation.1 | async-start | bytes 1769472 | tf_op jit(solution)/shard_map/all_gather | solution.py:116
  9.0 7.0 collective-permute-start
  13.3 708.7 %reduce-scatter.4.cloned.1.call-start = ((), (), s32[]{:S(2)}) async-start(), calls=%async_computation.2 | async-start | bytes 3170304
  16.0 10.3 %collective-permute-start.1 = (bf16[256,256]{1,0:T(8,128)(2,1)S(1)}, bf16[256,256]{1,0:T(8,128)(2,1)S(1)}, u32[]{:S(2)}, u32[]{:S(2)}) collective-permute-start(bf16[256,256]{1,0:T(8,128)(2,1)S(1)} %collective-permute-done), channel_id=1, source_target_pairs={{0,8},{8,16},{16,24},{24,32},{32,40},{40,48},{48,56},{56,64},{64,7... | collective-permute-start | bytes 393224 | tf_op jit(solution)/shard_map/ppermute | solution.py:15
  26.3 6.8 collective-permute-start.2
  33.1 6.8 copy-start.4
  38.2 1.7 copy-start
  41.0 1.8 copy-start.2
  44.0 8.3 %collective-permute-start.3 = (bf16[256,256]{0,1:T(8,128)(2,1)S(1)}, bf16[256,256]{0,1:T(8,128)(2,1)S(1)}, u32[]{:S(2)}, u32[]{:S(2)}) collective-permute-start(bf16[256,256]{0,1:T(8,128)(2,1)S(1)} %bitcast.247), channel_id=1, source_target_pairs={{8,0},{16,8},{24,16},{32,24},{40,32},{48,40},{56,48},{64,56},{72,6... | collective-permute-start | bytes 393224 | tf_op jit(solution)/shard_map/ppermute | solution.py:15
  45.3 14.2 %collective-permute-start.4 = (bf16[256,256]{0,1:T(8,128)(2,1)S(1)}, bf16[256,256]{0,1:T(8,128)(2,1)S(1)}, u32[]{:S(2)}, u32[]{:S(2)}) collective-permute-start(bf16[256,256]{0,1:T(8,128)(2,1)S(1)} %bitcast.246), channel_id=1, source_target_pairs={{16,0},{24,8},{32,16},{40,24},{48,32},{56,40},{64,48},{72,56},{80,... | collective-permute-start | bytes 393224 | tf_op jit(solution)/shard_map/ppermute | solution.py:15
  46.6 19.6 %collective-permute-start.5 = (bf16[256,256]{0,1:T(8,128)(2,1)S(1)}, bf16[256,256]{0,1:T(8,128)(2,1)S(1)}, u32[]{:S(2)}, u32[]{:S(2)}) collective-permute-start(bf16[256,256]{0,1:T(8,128)(2,1)S(1)} %bitcast.245), channel_id=1, source_target_pairs={{24,0},{32,8},{40,16},{48,24},{56,32},{64,40},{72,48},{80,56},{88,... | collective-permute-start | bytes 393224 | tf_op jit(solution)/shard_map/ppermute | solution.py:15
  70.7 1.4 copy-start.3
  70.7 3.6 copy-start.1
Sparse Core Ops, SparseCore 0:
  13.4 51.2 all-gather.1
  70.8 651.1 reduce-scatter.3
where the time goes:
time: 729 us
  waiting for transfers between devices  667 us (91%)
  starting transfers between devices  16.9 us (2%)
  between operations  14.4 us (2%)
  matrix products  14.1 us (2%)
  local copies, waits for them, and re-layouts  13.4 us (2%)
    unnamed x3, waiting for transfers between devices  646 us
    ppermute x6, waiting for transfers between devices, passed_along(): lax.ppermute(value, axis, [(source, source + steps) for source in range(i...  21.3 us
    ppermute x6, starting transfers between devices, passed_along(): lax.ppermute(value, axis, [(source, source + steps) for source in range(i...  16.8 us
  transfers between devices with their start and end apart: 8, of which 6 were waited for; matrix products, arithmetic and copies ran while one was open for 3% of the time, Pallas kernels for 0%

commit v1 on v0

--- a/solution.py
+++ b/solution.py
@@ -69,6 +69,25 @@
     )
 
 
+PARTS = 8
+DEPTH = 16
+STRIDED = [[part * DEPTH + z for part in range(PARTS)] for z in range(DEPTH)]
+RUNS = [[part * DEPTH + z for z in range(DEPTH)] for part in range(PARTS)]
+SWAP = [
+    ((i * DEPTH + z) * PARTS + j, (j * DEPTH + z) * PARTS + i)
+    for i in range(PARTS)
+    for z in range(DEPTH)
+    for j in range(PARTS)
+]
+
+
+def gathered_hidden(hidden_states):
+    column = lax.all_gather(
+        hidden_states, "tok", axis=0, tiled=True, axis_index_groups=STRIDED
+    )
+    return lax.ppermute(column, ("tok", "head"), SWAP)
+
+
 def body(
     queries_first,
     queries_second,
@@ -113,9 +132,14 @@
             block_term(back_steps).astype(jnp.bfloat16), "tok", -back_steps
         ).astype(jnp.float32)
     kv_grads = running.astype(jnp.bfloat16)
-    full_rows = lax.all_gather(hidden_states, "head", axis=1, tiled=True)
+    rows_here = gathered_hidden(hidden_states)
+    grads_here = lax.all_gather(kv_grads, "tok", axis=0, tiled=True, axis_index_groups=STRIDED)
     weight_grad = lax.psum_scatter(
-        projection_term(full_rows, kv_grads), "tok", scatter_dimension=0, tiled=True
+        projection_term(rows_here, grads_here),
+        "tok",
+        scatter_dimension=0,
+        tiled=True,
+        axis_index_groups=RUNS,
     )
     return (first_q, second_q, weight_grad)
 

time: 729 us -> 266 us (0.36)
  the two profiles are of different devices: /device:TPU:16 before, /device:TPU:56 now
where the time goes in v1:
time: 266 us; the launch traced here: 264 us
  waiting for transfers between devices  202 us (76%)
  starting transfers between devices  18.7 us (7%)
  matrix products  14.6 us (5%)
  between operations  14.1 us (5%)
  local copies, waits for them, and re-layouts  10.6 us (4%)
  other arithmetic  3.9 us (1%)
    all_gather x1, waiting for transfers between devices, body(): lax.all_gather(kv_grads, 'tok', axis=0, tiled=True, axis_index_groups=STR...  80.2 us
    unnamed x4, waiting for transfers between devices  65.1 us
    ppermute x6, waiting for transfers between devices, passed_along(): lax.ppermute(value, axis, [(source, source + steps) for source in range(i...  34.5 us
    ppermute x1, waiting for transfers between devices, gathered_hidden(): return lax.ppermute(column, ('tok', 'head'), SWAP)  22.5 us
    ppermute x6, starting transfers between devices, passed_along(): lax.ppermute(value, axis, [(source, source + steps) for source in range(i...  16.7 us
    unnamed x16, local copies, waits for them, and re-layouts  6.79 us
  transfers between devices with their start and end apart: 10, of which 9 were waited for; matrix products, arithmetic and copies ran while one was open for 9% of the time, Pallas kernels for 0%

profile of v1, /device:TPU:56, one launch (start us, length us, event | category | flops | bytes accessed | tf_op | source)
XLA Modules:
  0.0 264.1 jit_solution(16499803670144012279)
XLA Ops:
  7.2 0.9 constant_dynamic-update-slice_fusion.1
  8.1 0.9 constant_dynamic-update-slice_fusion
  9.0 4.3 %collective-permute-start = (bf16[256,256]{1,0:T(8,128)(2,1)S(1)}, bf16[256,256]{1,0:T(8,128)(2,1)S(1)}, u32[]{:S(2)}, u32[]{:S(2)}) collective-permute-start(bf16[256,256]{1,0:T(8,128)(2,1)S(1)} %constant_dynamic-update-slice_fusion), channel_id=1, source_target_pairs={{0,8},{8,16},{16,24},{24,32},{32,40},{40,48},{48,56},{56,64},{64,7... | collective-permute-start | bytes 393224 | tf_op jit(solution)/shard_map/ppermute | solution.py:15
  13.4 0.8 copy.89
  14.1 0.2 reduce-window.8
  14.3 0.1 reduce.6
  14.4 0.2 convert_reduce_fusion.1
  14.6 16.9 %collective-permute-done = bf16[256,256]{1,0:T(8,128)(2,1)S(1)} collective-permute-done((bf16[256,256]{1,0:T(8,128)(2,1)S(1)}, bf16[256,256]{1,0:T(8,128)(2,1)S(1)}, u32[]{:S(2)}, u32[]{:S(2)}) %collective-permute-start) | collective-permute-done | bytes 131104 | tf_op jit(solution)/shard_map/ppermute | solution.py:15
  31.5 1.9 collective-permute-start.1
  33.4 1.1 copy.101
  34.5 1.1 copy.103
  35.5 1.1 copy.92
  36.6 1.1 copy.94
  37.8 1.1 copy.90
  38.8 0.1 copy.99
  39.0 0.4 convert_reduce_fusion
  39.3 1.1 collective-permute-done.1
  40.4 1.9 collective-permute-start.2
  42.3 0.9 and_and_fusion
  43.3 6.2 %collective-permute-done.2 = bf16[256,256]{1,0:T(8,128)(2,1)S(1)} collective-permute-done((bf16[256,256]{1,0:T(8,128)(2,1)S(1)}, bf16[256,256]{1,0:T(8,128)(2,1)S(1)}, u32[]{:S(2)}, u32[]{:S(2)}) %collective-permute-start.2) | collective-permute-done | bytes 131104 | tf_op jit(solution)/shard_map/ppermute | solution.py:15
  49.5 0.6 fusion.91
  50.1 1.0 fusion.9
  51.1 1.3 fusion.7
  52.4 1.1 fusion.79
  53.5 1.1 fusion.3
  54.6 0.6 fusion.31
  55.3 1.1 fusion.82
  56.3 1.1 fusion.1
  57.5 0.7 fusion.46
  58.1 1.1 fusion.28
  59.3 1.1 fusion.52
  60.5 2.8 %collective-permute-start.3 = (bf16[256,256]{0,1:T(8,128)(2,1)S(1)}, bf16[256,256]{0,1:T(8,128)(2,1)S(1)}, u32[]{:S(2)}, u32[]{:S(2)}) collective-permute-start(bf16[256,256]{0,1:T(8,128)(2,1)S(1)} %bitcast.247), channel_id=1, source_target_pairs={{8,0},{16,8},{24,16},{32,24},{40,32},{48,40},{56,48},{64,56},{72,6... | collective-permute-start | bytes 393224 | tf_op jit(solution)/shard_map/ppermute | solution.py:15
  63.2 1.9 collective-permute-start.4
  65.2 3.9 %collective-permute-start.5 = (bf16[256,256]{0,1:T(8,128)(2,1)S(1)}, bf16[256,256]{0,1:T(8,128)(2,1)S(1)}, u32[]{:S(2)}, u32[]{:S(2)}) collective-permute-start(bf16[256,256]{0,1:T(8,128)(2,1)S(1)} %bitcast.245), channel_id=1, source_target_pairs={{24,0},{32,8},{40,16},{48,24},{56,32},{64,40},{72,48},{80,56},{88,... | collective-permute-start | bytes 393224 | tf_op jit(solution)/shard_map/ppermute | solution.py:15
  69.1 2.0 collective-permute-done.3
  71.2 6.6 %collective-permute-done.4 = bf16[256,256]{0,1:T(8,128)(2,1)S(1)} collective-permute-done((bf16[256,256]{0,1:T(8,128)(2,1)S(1)}, bf16[256,256]{0,1:T(8,128)(2,1)S(1)}, u32[]{:S(2)}, u32[]{:S(2)}) %collective-permute-start.4) | collective-permute-done | bytes 131104 | tf_op jit(solution)/shard_map/ppermute | solution.py:15
  77.8 1.7 collective-permute-done.5
  79.5 0.7 fusion.89
  80.3 1.9 collective-permute-start.6
  82.2 80.2 %all-gather.3.cloned.1.call-done = bf16[2048,256]{0,1:T(8,128)(2,1)} async-done(((bf16[256,256]{0,1:T(8,128)(2,1)}), bf16[2048,256]{0,1:T(8,128)(2,1)}) %all-gather.3.cloned.1.call-update) | async-done | bytes 1048592 | tf_op jit(solution)/shard_map/all_gather | solution.py:136
  162.4 22.5 %collective-permute-done.6 = bf16[2048,384]{1,0:T(8,128)(2,1)} collective-permute-done((bf16[2048,384]{1,0:T(8,128)(2,1)}, bf16[2048,384]{1,0:T(8,128)(2,1)}, u32[]{:S(2)}, u32[]{:S(2)}) %collective-permute-start.6) | collective-permute-done | bytes 1572896 | tf_op jit(solution)/shard_map/ppermute | solution.py:88
  184.9 2.4 convolution_bitcast_fusion
  187.3 0.9 copy.135
  188.2 1.4 fusion.73
  189.6 0.8 copy.113
  190.4 1.4 fusion.76
  191.8 0.8 copy.112
  192.6 65.0 %reduce-scatter.4.cloned.1.call-done = f32[24,256]{1,0:T(8,128)} async-done(((f32[384,256]{1,0:T(8,128)}), f32[24,256]{1,0:T(8,128)}) %reduce-scatter.4.cloned.1.call-update) | async-done | bytes 24592
  (23 shorter events, 0.4 us)
Async XLA Ops:
  7.2 31.7 %copy-start.1 = (bf16[256,384]{1,0:T(8,128)(2,1)S(1)}, bf16[256,384]{1,0:T(8,128)(2,1)}, u32[]{:S(2)}) copy-start(bf16[256,384]{1,0:T(8,128)(2,1)} %param.9) | copy-start | bytes 589828
  7.2 73.1 %all-gather.5.cloned.1.call-start = ((), (), s32[]{:S(2)}) async-start(), calls=%async_computation.2 | async-start | bytes 1769472 | tf_op jit(solution)/shard_map/all_gather | solution.py:85
  9.0 22.5 %collective-permute-start = (bf16[256,256]{1,0:T(8,128)(2,1)S(1)}, bf16[256,256]{1,0:T(8,128)(2,1)S(1)}, u32[]{:S(2)}, u32[]{:S(2)}) collective-permute-start(bf16[256,256]{1,0:T(8,128)(2,1)S(1)} %constant_dynamic-update-slice_fusion), channel_id=1, source_target_pairs={{0,8},{8,16},{16,24},{24,32},{32,40},{40,48},{48,56},{56,64},{64,7... | collective-permute-start | bytes 393224 | tf_op jit(solution)/shard_map/ppermute | solution.py:15
  13.3 149.1 %all-gather.3.cloned.1.call-start = ((), (), s32[]{:S(2)}) async-start(), calls=%async_computation.1 | async-start | bytes 1179648 | tf_op jit(solution)/shard_map/all_gather | solution.py:136
  31.5 9.0 %collective-permute-start.1 = (bf16[256,256]{1,0:T(8,128)(2,1)S(1)}, bf16[256,256]{1,0:T(8,128)(2,1)S(1)}, u32[]{:S(2)}, u32[]{:S(2)}) collective-permute-start(bf16[256,256]{1,0:T(8,128)(2,1)S(1)} %collective-permute-done), channel_id=1, source_target_pairs={{0,8},{8,16},{16,24},{24,32},{32,40},{40,48},{48,56},{56,64},{64,7... | collective-permute-start | bytes 393224 | tf_op jit(solution)/shard_map/ppermute | solution.py:15
  36.6 16.9 %copy-start.2 = (bf16[256,384]{0,1:T(8,128)(2,1)}, bf16[256,384]{0,1:T(8,128)(2,1)S(1)}, u32[]{:S(2)}) copy-start(bf16[256,384]{0,1:T(8,128)(2,1)S(1)} %copy.92) | copy-start | bytes 589828
  40.4 9.1 %collective-permute-start.2 = (bf16[256,256]{1,0:T(8,128)(2,1)S(1)}, bf16[256,256]{1,0:T(8,128)(2,1)S(1)}, u32[]{:S(2)}, u32[]{:S(2)}) collective-permute-start(bf16[256,256]{1,0:T(8,128)(2,1)S(1)} %collective-permute-done.1), channel_id=1, source_target_pairs={{0,8},{8,16},{16,24},{24,32},{32,40},{40,48},{48,56},{56,64},{64,7... | collective-permute-start | bytes 393224 | tf_op jit(solution)/shard_map/ppermute | solution.py:15
  49.5 6.8 %copy-start = (bf16[1024,256]{1,0:T(8,128)(2,1)}, bf16[1024,256]{1,0:T(8,128)(2,1)S(1)}, u32[]{:S(2)}) copy-start(bf16[1024,256]{1,0:T(8,128)(2,1)S(1)} %pad_maximum_fusion.1) | copy-start | bytes 1572868
  56.3 1.8 copy-start.3
  60.5 10.7 %collective-permute-start.3 = (bf16[256,256]{0,1:T(8,128)(2,1)S(1)}, bf16[256,256]{0,1:T(8,128)(2,1)S(1)}, u32[]{:S(2)}, u32[]{:S(2)}) collective-permute-start(bf16[256,256]{0,1:T(8,128)(2,1)S(1)} %bitcast.247), channel_id=1, source_target_pairs={{8,0},{16,8},{24,16},{32,24},{40,32},{48,40},{56,48},{64,56},{72,6... | collective-permute-start | bytes 393224 | tf_op jit(solution)/shard_map/ppermute | solution.py:15
  63.2 14.5 %collective-permute-start.4 = (bf16[256,256]{0,1:T(8,128)(2,1)S(1)}, bf16[256,256]{0,1:T(8,128)(2,1)S(1)}, u32[]{:S(2)}, u32[]{:S(2)}) collective-permute-start(bf16[256,256]{0,1:T(8,128)(2,1)S(1)} %bitcast.246), channel_id=1, source_target_pairs={{16,0},{24,8},{32,16},{40,24},{48,32},{56,40},{64,48},{72,56},{80,... | collective-permute-start | bytes 393224 | tf_op jit(solution)/shard_map/ppermute | solution.py:15
  65.2 14.3 %collective-permute-start.5 = (bf16[256,256]{0,1:T(8,128)(2,1)S(1)}, bf16[256,256]{0,1:T(8,128)(2,1)S(1)}, u32[]{:S(2)}, u32[]{:S(2)}) collective-permute-start(bf16[256,256]{0,1:T(8,128)(2,1)S(1)} %bitcast.245), channel_id=1, source_target_pairs={{24,0},{32,8},{40,16},{48,24},{56,32},{64,40},{72,48},{80,56},{88,... | collective-permute-start | bytes 393224 | tf_op jit(solution)/shard_map/ppermute | solution.py:15
  80.2 177.4 %reduce-scatter.4.cloned.1.call-start = ((), (), s32[]{:S(2)}) async-start(), calls=%async_computation.3 | async-start | bytes 417792
  80.3 104.6 %collective-permute-start.6 = (bf16[2048,384]{1,0:T(8,128)(2,1)}, bf16[2048,384]{1,0:T(8,128)(2,1)}, u32[]{:S(2)}, u32[]{:S(2)}) collective-permute-start(bf16[2048,384]{1,0:T(8,128)(2,1)} %all-gather.5.cloned.1.call-done), channel_id=1, source_target_pairs={{0,0},{1,128},{2,256},{3,384},{4,512},{5,640},{6,768},{7,896},{8,8... | collective-permute-start | bytes 4718600 | tf_op jit(solution)/shard_map/ppermute | solution.py:88
Sparse Core Ops, SparseCore 0:
  13.4 61.0 all-gather.4
  80.3 81.9 all-gather.2
  188.3 69.2 reduce-scatter.3

commit v2 on v0

v2 whole, which is shorter than its diff:
```python
import math

import jax
import jax.numpy as jnp
from jax import lax
from jax.experimental import pallas as pl
from jax.experimental.pallas import tpu as pltpu
from jax.sharding import PartitionSpec as P

HD = 128
ROWS = 256
GROUP = 3
LAYERS = 2
PAIRS = LAYERS * GROUP
WIDTH = GROUP * HD
WINDOW = 4
NX = 4
NYL = 2
NZ = 16
NYH = 4
NCORE = 2
TOKS = NX * NYL * NZ
SLOTS = NX * NYL
OUT_ROWS = WIDTH // NZ
SCALE = 1.0 / math.sqrt(HD)
MASKED = -1e30
MESH = pl.DeviceIdType.MESH
F32 = jnp.float32
BF16 = jnp.bfloat16
FAR_FIRST = sorted(range(1, NZ), key=lambda d: -min(d, NZ - d))


def dot_nt(a, b):
    return lax.dot_general(a, b, (((1,), (1,)), ((), ())), preferred_element_type=F32)


def dot_nn(a, b):
    return lax.dot_general(a, b, (((1,), (0,)), ((), ())), preferred_element_type=F32)


def kernel(
    q1_in, q2_in, g1_in, g2_in, k_in, v_in, hid_in, docs,
    dq1_out, dq2_out, wg_out,
    qv, gv, kvb, e, dp, bias, st_m, st_l, st_d, fac, delta, acck, accv, dqt, dqv,
    gs, gr, s1, a2, a3, at, bb, st, rs,
    in_sem, out_sem, halo_send, halo_recv, grad_send, grad_recv,
    s1_send, s1_recv, s2_send, s2_recv, s3_send, s3_recv,
    b_send, b_recv, rs_send, rs_recv,
):
    t = lax.axis_index("tok")
    h = lax.axis_index("head")
    z = lax.rem(t, NZ)
    i = lax.div(t, NZ)
    yl = lax.rem(i, NYL)
    x = lax.div(i, NYL)
    core = lax.rem(h, NCORE)
    yh = lax.div(h, NCORE)

    def tok_of(xx, yy, zz):
        return (xx * NYL + yy) * NZ + zz

    t_next = lax.rem(t + 1, TOKS)
    t_prev = lax.rem(t + TOKS - 1, TOKS)
    sibling = h + 1 - 2 * core
    y_pair = tok_of(x, 1 - yl, z)

    def x_tok(step):
        return tok_of(lax.rem(x + step, NX), yl, z)

    def z_tok(step):
        return i * NZ + lax.rem(z + step, NZ)

    def fan_id(step):
        return (tok_of(x, core, z), lax.rem(yh + step, NYH) * NCORE + yl)

    crossed = yl != core

    def send(src, dst, send_sem, recv_sem, where):
        return pltpu.make_async_remote_copy(
            src_ref=src, dst_ref=dst, send_sem=send_sem, recv_sem=recv_sem,
            device_id=where, device_id_type=MESH,
        )

    loads = [
        pltpu.make_async_copy(k_in, kvb.at[3, 0], in_sem.at[0]),
        pltpu.make_async_copy(v_in, kvb.at[3, 1], in_sem.at[1]),
        pltpu.make_async_copy(q1_in, qv.at[0], in_sem.at[2]),
        pltpu.make_async_copy(q2_in, qv.at[1], in_sem.at[3]),
        pltpu.make_async_copy(g1_in, gv.at[0], in_sem.at[4]),
        pltpu.make_async_copy(g2_in, gv.at[1], in_sem.at[5]),
    ]
    for load in loads:
        load.start()

    barrier = pltpu.get_barrier_semaphore()

    def greet(where):
        pl.semaphore_signal(barrier, inc=1, device_id=where, device_id_type=MESH)

    for d in FAR_FIRST:
        greet((z_tok(d), h))
    for d in range(1, NYH):
        greet(fan_id(d))

    @pl.when(crossed)
    def _():
        greet(fan_id(0))

    for d in range(1, NX):
        greet((x_tok(d), h))
    greet((y_pair, h))
    greet((t_next, h))
    greet((t_prev, h))
    greet((t, sibling))

    lengths = docs[...].astype(F32)
    row = lax.broadcasted_iota(jnp.int32, (128, 128), 0)
    col = lax.broadcasted_iota(jnp.int32, (128, 128), 1)
    ends = jnp.sum(jnp.where(col <= row, lengths, 0.0), axis=1, keepdims=True)
    base = (t * ROWS).astype(F32)
    place = base + lax.broadcasted_iota(jnp.int32, (128, ROWS), 1).astype(F32)
    first = jnp.max(jnp.where(ends <= place, ends, 0.0), axis=0, keepdims=True)
    first = (first - base).astype(jnp.int32) + (WINDOW - 1) * ROWS

    pl.semaphore_wait(barrier, 15 + 3 + 3 + 1 + 2 + 1 + lax.rem(yl + core, 2))

    def halo(hop, s):
        src = (k_in, v_in)[s] if hop == 0 else kvb.at[3 - hop, s]
        return send(
            src, kvb.at[2 - hop, s], halo_send.at[hop, s], halo_recv.at[hop, s], (t_next, h)
        )

    def fan(step):
        return send(hid_in, s1.at[step], s1_send.at[step], s1_recv.at[step], fan_id(step))

    halo(0, 0).start()
    halo(0, 1).start()
    for d in (2, 1, 3):
        fan(d).start()

    @pl.when(crossed)
    def _():
        fan(0).start()

    @pl.when(jnp.logical_not(crossed))
    def _():
        pltpu.make_async_copy(hid_in, s1.at[0], s1_recv.at[0]).start()

    for load in loads:
        load.wait()

    key_row = lax.broadcasted_iota(jnp.int32, (ROWS, ROWS), 0)
    query_col = lax.broadcasted_iota(jnp.int32, (ROWS, ROWS), 1)

    def scores_of(b):
        seen = key_row + b * ROWS >= first
        if b == WINDOW - 1:
            seen = seen & (key_row <= query_col)
        bias[...] = jnp.where(seen, 0.0, MASKED)

        def one_head(g, carry):
            cols = pl.ds(pl.multiple_of(g * HD, HD), HD)
            for layer in range(LAYERS):
                pair = layer * GROUP + g
                s = dot_nt(kvb[b, 0], qv[layer, :, cols]) * SCALE + bias[...]
                top = jnp.max(s, axis=0, keepdims=True)
                raised = jnp.exp(s - top)
                grad = dot_nt(kvb[b, 1], gv[layer, :, cols])
                e[b, pair] = raised
                dp[b, pair] = grad
                st_m[b, pair] = top
                st_l[b, pair] = jnp.sum(raised, axis=0, keepdims=True)
                st_d[b, pair] = jnp.sum(raised * grad, axis=0, keepdims=True)
            return carry

        lax.fori_loop(0, GROUP, one_head, 0)

    scores_of(3)
    for hop in range(2):
        for s in range(2):
            halo(hop, s).wait_recv()
            halo(hop + 1, s).start()
        scores_of(2 - hop)
    for s in range(2):
        halo(2, s).wait_recv()
    scores_of(0)

    for pair in range(PAIRS):
        top = st_m[0, pair]
        for b in range(1, WINDOW):
            top = jnp.maximum(top, st_m[b, pair])
        weights = [jnp.exp(st_m[b, pair] - top) for b in range(WINDOW)]
        total = weights[0] * st_l[0, pair]
        moved = weights[0] * st_d[0, pair]
        for b in range(1, WINDOW):
            total = total + weights[b] * st_l[b, pair]
            moved = moved + weights[b] * st_d[b, pair]
        inverse = 1.0 / total
        delta[pair] = moved * inverse
        for b in range(WINDOW):
            fac[b, pair] = weights[b] * inverse

    def grads_of(b):
        keys_t = jnp.transpose(kvb[b, 0])
        accv[...] = jnp.zeros_like(accv)
        acck[...] = jnp.zeros_like(acck)

        def one_head(g, carry):
            cols = pl.ds(pl.multiple_of(g * HD, HD), HD)
            for layer in range(LAYERS):
                pair = layer * GROUP + g
                probs = e[b, pair] * fac[b, pair]
                shift = (probs * (dp[b, pair] - delta[pair])).astype(BF16)
                accv[...] += dot_nn(probs.astype(BF16), gv[layer, :, cols])
                acck[...] += dot_nn(shift, qv[layer, :, cols])
                term = dot_nn(keys_t, shift)
                if b == 0:
                    dqt[pair] = term
                else:
                    dqt[pair] += term
            return carry

        lax.fori_loop(0, GROUP, one_head, 0)

    def pass_back(b, s):
        return send(
            gs.at[b, s], gr.at[b, s], grad_send.at[b, s], grad_recv.at[b, s], (t_prev, h)
        )

    def hand_over(b, s):
        mine = accv[...] if s == 1 else acck[...] * SCALE
        if b > 0:
            pass_back(b - 1, s).wait_recv()
            mine = mine + gr[b - 1, s].astype(F32)
        if b < WINDOW - 1:
            gs[b, s] = mine.astype(BF16)
            pass_back(b, s).start()
        else:
            bb[s, 0] = mine.astype(BF16)

    def column_slot(step):
        return lax.rem(yh + 2 * NX - x - step, NX)

    def across(step):
        return send(
            s1.at[column_slot(step)], a2.at[step], s2_send.at[step], s2_recv.at[step],
            (x_tok(step), h),
        )

    def own_block(step):
        return s1.at[column_slot(0)] if step == 0 else a2.at[step]

    def share(step):
        return send(
            own_block(step), a3.at[step], s3_send.at[step], s3_recv.at[step], (t, sibling)
        )

    grads_of(0)
    hand_over(0, 1)
    hand_over(0, 0)
    grads_of(1)
    hand_over(1, 1)
    hand_over(1, 0)
    for step in (2, 1, 3, 0):
        slot = column_slot(step)
        send(
            hid_in, s1.at[slot], s1_send.at[slot], s1_recv.at[slot], (t_next, h)
        ).wait_recv()
        if step:
            across(step).start()
    grads_of(2)
    hand_over(2, 1)
    hand_over(2, 0)
    grads_of(3)

    for pair in range(PAIRS):
        layer, g = divmod(pair, GROUP)
        dqv[layer, :, g * HD : (g + 1) * HD] = (jnp.transpose(dqt[pair]) * SCALE).astype(BF16)
    stores = [
        pltpu.make_async_copy(dqv.at[0], dq1_out, out_sem.at[0]),
        pltpu.make_async_copy(dqv.at[1], dq2_out, out_sem.at[1]),
    ]
    for store in stores:
        store.start()

    def spread(s, src, dst, where):
        return send(
            bb.at[s, src], bb.at[s, dst], b_send.at[s, dst], b_recv.at[s, dst], (where, h)
        )

    def from_pair(s):
        return spread(s, 0, 1, y_pair)

    def own_up(s):
        return spread(s, 0, 2, x_tok(1))

    def own_down(s):
        return spread(s, 0, 6, x_tok(3))

    def pair_up(s):
        return spread(s, 1, 3, x_tok(1))

    def pair_down(s):
        return spread(s, 1, 7, x_tok(3))

    def own_far(s):
        return spread(s, 2, 4, x_tok(1))

    def pair_far(s):
        return spread(s, 7, 5, x_tok(3))

    for s in (1, 0):
        hand_over(3, s)
        from_pair(s).start()
        own_up(s).start()
        own_down(s).start()

    share(0).start()
    for step in range(1, NX):
        across(step).wait_recv()
        share(step).start()

    for s in (1, 0):
        from_pair(s).wait_recv()
        pair_down(s).start()
        pair_up(s).start()
        own_up(s).wait_recv()
        own_far(s).start()

    def slot_of(step, dy):
        return step * NYL + dy

    near = lax.rem(yl + core, 2)
    at[near] = jnp.transpose(s1[column_slot(0)])
    for step in range(1, NX):
        at[slot_of(step, near)] = jnp.transpose(a2[step])

    for s in (1, 0):
        pair_down(s).wait_recv()
        pair_far(s).start()

    for step in range(NX):
        share(step).wait_recv()
        at[slot_of(step, 1 - near)] = jnp.transpose(a3[step])

    def scatter(s, step):
        return send(
            st.at[s, lax.rem(z + step, NZ)], rs.at[s, step], rs_send.at[s, step],
            rs_recv.at[s, step], (z_tok(step), h),
        )

    for s in (1, 0):
        for landed in (own_down, pair_up, own_far, pair_far):
            landed(s).wait_recv()
        total = dot_nn(at[0], bb[s, 0])
        for slot in range(1, SLOTS):
            total = total + dot_nn(at[slot], bb[s, slot])
        st[s] = total.reshape(NZ, OUT_ROWS, HD).astype(BF16)
        for step in FAR_FIRST:
            scatter(s, step).start()

    for s in (1, 0):
        summed = st[s, z].astype(F32)
        for step in range(1, NZ):
            scatter(s, step).wait_recv()
            summed = summed + rs[s, step].astype(F32)
        wg_out[:, s * HD : (s + 1) * HD] = summed

    for store in stores:
        store.wait()
    for hop in range(3):
        for s in range(2):
            halo(hop, s).wait_send()
            pass_back(hop, s).wait_send()
    for step in range(1, NYH):
        fan(step).wait_send()

    @pl.when(crossed)
    def _():
        fan(0).wait_send()

    for step in range(NX):
        if step:
            across(step).wait_send()
        share(step).wait_send()
    for s in range(2):
        for sent in (from_pair, own_up, own_down, pair_up, pair_down, own_far, pair_far):
            sent(s).wait_send()
        for step in range(1, NZ):
            scatter(s, step).wait_send()


def body(
    queries_first,
    queries_second,
    grads_first,
    grads_second,
    key_states,
    value_states,
    doc_lengths,
    hidden_states,
):
    anywhere = pl.BlockSpec(memory_space=pl.ANY)
    in_vmem = pl.BlockSpec(memory_space=pltpu.VMEM)
    dma = pltpu.SemaphoreType.DMA
    vmem = pltpu.VMEM
    return pl.pallas_call(
        kernel,
        out_shape=(
            jax.ShapeDtypeStruct((ROWS, WIDTH), BF16),
            jax.ShapeDtypeStruct((ROWS, WIDTH), BF16),
            jax.ShapeDtypeStruct((OUT_ROWS, 2 * HD), F32),
        ),
        in_specs=[anywhere] * 7 + [in_vmem],
        out_specs=(anywhere, anywhere, in_vmem),
        scratch_shapes=[
            vmem((LAYERS, ROWS, WIDTH), BF16),
            vmem((LAYERS, ROWS, WIDTH), BF16),
            vmem((WINDOW, 2, ROWS, HD), BF16),
            vmem((WINDOW, PAIRS, ROWS, ROWS), F32),
            vmem((WINDOW, PAIRS, ROWS, ROWS), F32),
            vmem((ROWS, ROWS), F32),
            vmem((WINDOW, PAIRS, 1, ROWS), F32),
            vmem((WINDOW, PAIRS, 1, ROWS), F32),
            vmem((WINDOW, PAIRS, 1, ROWS), F32),
            vmem((WINDOW, PAIRS, 1, ROWS), F32),
            vmem((PAIRS, 1, ROWS), F32),
            vmem((ROWS, HD), F32),
            vmem((ROWS, HD), F32),
            vmem((PAIRS, HD, ROWS), F32),
            vmem((LAYERS, ROWS, WIDTH), BF16),
            vmem((WINDOW - 1, 2, ROWS, HD), BF16),
            vmem((WINDOW - 1, 2, ROWS, HD), BF16),
            vmem((NYH, ROWS, WIDTH), BF16),
            vmem((NX, ROWS, WIDTH), BF16),
            vmem((NX, ROWS, WIDTH), BF16),
            vmem((SLOTS, WIDTH, ROWS), BF16),
            vmem((2, SLOTS, ROWS, HD), BF16),
            vmem((2, NZ, OUT_ROWS, HD), BF16),
            vmem((2, NZ, OUT_ROWS, HD), BF16),
            dma((6,)), dma((2,)), dma((3, 2)), dma((3, 2)), dma((3, 2)), dma((3, 2)),
            dma((NYH,)), dma((NYH,)), dma((NX,)), dma((NX,)), dma((NX,)), dma((NX,)),
            dma((2, SLOTS)), dma((2, SLOTS)), dma((2, NZ)), dma((2, NZ)),
        ],
        compiler_params=pltpu.CompilerParams(
            collective_id=0, has_side_effects=True, vmem_limit_bytes=48 << 20
        ),
    )(
        queries_first,
        queries_second,
        grads_first,
        grads_second,
        key_states,
        value_states,
        hidden_states,
        doc_lengths.reshape(1, 128),
    )


def solution(mesh):
    spread = P("tok", "head")
    return jax.shard_map(
        body,
        mesh=mesh,
        in_specs=(spread,) * 6 + (P(), spread),
        out_specs=(spread, spread, spread),
        check_vma=False,
    )
```

time: 729 us -> 86 us (0.12)
  the two profiles are of different devices: /device:TPU:16 before, /device:TPU:10 now
where the time goes in v2:
time: 86 us; the launch traced here: 85.7 us
  Pallas kernels  76.1 us (88%)
  local copies, waits for them, and re-layouts  8.92 us (10%)
    pallas_call x1, Pallas kernels, body(): pl.pallas_call(kernel, out_shape=(jax.ShapeDtypeStruct((ROWS, WIDTH), BF1...  76.1 us
    unnamed x19, local copies, waits for them, and re-layouts  8.92 us

profile of v2, /device:TPU:10, one launch (start us, length us, event | category | flops | bytes accessed | tf_op | source)
XLA Modules:
  0.0 85.7 jit_solution(6800666545116547510)
XLA Ops:
  0.6 0.0 copy-start.7
  0.6 0.6 copy-done.7
  1.3 0.0 copy-start
  1.3 0.9 %copy-done = bf16[256,384]{1,0:T(8,128)(2,1)S(1)} copy-done((bf16[256,384]{1,0:T(8,128)(2,1)S(1)}, bf16[256,384]{1,0:T(8,128)(2,1)}, u32[]{:S(2)}) %copy-start) | copy-done | bytes 196632
  2.2 0.0 copy-start.1
  2.2 0.9 %copy-done.1 = bf16[256,384]{1,0:T(8,128)(2,1)S(1)} copy-done((bf16[256,384]{1,0:T(8,128)(2,1)S(1)}, bf16[256,384]{1,0:T(8,128)(2,1)}, u32[]{:S(2)}) %copy-start.1) | copy-done | bytes 196632
  3.1 0.0 copy-start.2
  3.1 0.9 %copy-done.2 = bf16[256,384]{1,0:T(8,128)(2,1)S(1)} copy-done((bf16[256,384]{1,0:T(8,128)(2,1)S(1)}, bf16[256,384]{1,0:T(8,128)(2,1)}, u32[]{:S(2)}) %copy-start.2) | copy-done | bytes 196632
  4.1 0.0 copy-start.3
  4.1 0.9 %copy-done.3 = bf16[256,384]{1,0:T(8,128)(2,1)S(1)} copy-done((bf16[256,384]{1,0:T(8,128)(2,1)S(1)}, bf16[256,384]{1,0:T(8,128)(2,1)}, u32[]{:S(2)}) %copy-start.3) | copy-done | bytes 196632
  5.0 0.0 copy-start.4
  5.0 0.9 %copy-done.4 = bf16[256,384]{1,0:T(8,128)(2,1)S(1)} copy-done((bf16[256,384]{1,0:T(8,128)(2,1)S(1)}, bf16[256,384]{1,0:T(8,128)(2,1)}, u32[]{:S(2)}) %copy-start.4) | copy-done | bytes 196632
  5.9 0.0 copy-start.5
  5.9 0.8 copy-done.5
  6.8 0.0 copy-start.6
  6.8 0.8 copy-done.6
  7.6 76.1 %shard_map.103 = (bf16[256,384]{1,0:T(8,128)(2,1)S(1)}, bf16[256,384]{1,0:T(8,128)(2,1)S(1)}, f32[24,256]{1,0:T(8,128)S(1)}) custom-call(bf16[256,384]{1,0:T(8,128)(2,1)S(1)} %copy-done, bf16[256,384]{1,0:T(8,128)(2,1)S(1)} %copy-done.1, bf16[256,384]{1,0:T(8,128)(2,1)S(1)} %copy-done.2, bf16[256,384]{1,0:T(8,128)(2,1)S(1)} %copy-done.3, ...), custom_call_target="tpu_custom_call" | custom-call | tf_op jit(solution)/shard_map/pallas_call | solution.py:407
  83.7 0.7 copy.14
  84.4 0.7 copy.15
  85.1 0.6 copy.16
Async XLA Ops:
  0.6 0.7 copy-start.7
  1.3 0.9 %copy-start = (bf16[256,384]{1,0:T(8,128)(2,1)S(1)}, bf16[256,384]{1,0:T(8,128)(2,1)}, u32[]{:S(2)}) copy-start(bf16[256,384]{1,0:T(8,128)(2,1)} %q1_in.1) | copy-start | bytes 589828
  2.2 0.9 %copy-start.1 = (bf16[256,384]{1,0:T(8,128)(2,1)S(1)}, bf16[256,384]{1,0:T(8,128)(2,1)}, u32[]{:S(2)}) copy-start(bf16[256,384]{1,0:T(8,128)(2,1)} %q2_in.1) | copy-start | bytes 589828
  3.1 0.9 %copy-start.2 = (bf16[256,384]{1,0:T(8,128)(2,1)S(1)}, bf16[256,384]{1,0:T(8,128)(2,1)}, u32[]{:S(2)}) copy-start(bf16[256,384]{1,0:T(8,128)(2,1)} %g1_in.1) | copy-start | bytes 589828
  4.1 0.9 %copy-start.3 = (bf16[256,384]{1,0:T(8,128)(2,1)S(1)}, bf16[256,384]{1,0:T(8,128)(2,1)}, u32[]{:S(2)}) copy-start(bf16[256,384]{1,0:T(8,128)(2,1)} %g2_in.1) | copy-start | bytes 589828
  5.0 0.9 %copy-start.4 = (bf16[256,384]{1,0:T(8,128)(2,1)S(1)}, bf16[256,384]{1,0:T(8,128)(2,1)}, u32[]{:S(2)}) copy-start(bf16[256,384]{1,0:T(8,128)(2,1)} %hid_in.1) | copy-start | bytes 589828
  5.9 0.8 copy-start.5
  6.8 0.8 copy-start.6

commit v3 on v2

--- a/solution.py
+++ b/solution.py
@@ -44,7 +44,7 @@
     qv, gv, kvb, e, dp, bias, st_m, st_l, st_d, fac, delta, acck, accv, dqt, dqv,
     gs, gr, s1, a2, a3, at, bb, st, rs,
     in_sem, out_sem, halo_send, halo_recv, grad_send, grad_recv,
-    s1_send, s1_recv, s2_send, s2_recv, s3_send, s3_recv,
+    s1_send, s1_recv, relay_send, s2_send, s2_recv, s3_send, s3_recv,
     b_send, b_recv, rs_send, rs_recv,
 ):
     t = lax.axis_index("tok")
@@ -73,7 +73,14 @@
     def fan_id(step):
         return (tok_of(x, core, z), lax.rem(yh + step, NYH) * NCORE + yl)
 
+    case_same_low = jnp.logical_and(yl == 0, core == 0)
+    case_same_high = jnp.logical_and(yl == 1, core == 1)
+    case_low_high = jnp.logical_and(yl == 0, core == 1)
+    case_high_low = jnp.logical_and(yl == 1, core == 0)
     crossed = yl != core
+
+    def head_at(step):
+        return lax.rem(yh + step, NYH) * NCORE + core
 
     def send(src, dst, send_sem, recv_sem, where):
         return pltpu.make_async_remote_copy(
@@ -112,6 +119,8 @@
     greet((t_next, h))
     greet((t_prev, h))
     greet((t, sibling))
+    greet((t, head_at(1)))
+    greet((t, head_at(NYH - 1)))
 
     lengths = docs[...].astype(F32)
     row = lax.broadcasted_iota(jnp.int32, (128, 128), 0)
@@ -122,7 +131,7 @@
     first = jnp.max(jnp.where(ends <= place, ends, 0.0), axis=0, keepdims=True)
     first = (first - base).astype(jnp.int32) + (WINDOW - 1) * ROWS
 
-    pl.semaphore_wait(barrier, 15 + 3 + 3 + 1 + 2 + 1 + lax.rem(yl + core, 2))
+    pl.semaphore_wait(barrier, 15 + 3 + 3 + 1 + 2 + 1 + 2 + lax.rem(yl + core, 2))
 
     def halo(hop, s):
         src = (k_in, v_in)[s] if hop == 0 else kvb.at[3 - hop, s]
@@ -135,12 +144,23 @@
 
     halo(0, 0).start()
     halo(0, 1).start()
-    for d in (2, 1, 3):
-        fan(d).start()
-
-    @pl.when(crossed)
-    def _():
-        fan(0).start()
+    def sends(act):
+        @pl.when(jnp.logical_not(crossed))
+        def _():
+            act(1)
+            act(3)
+
+        @pl.when(case_low_high)
+        def _():
+            act(0)
+            act(3)
+
+        @pl.when(case_high_low)
+        def _():
+            act(0)
+            act(1)
+
+    sends(lambda step: fan(step).start())
 
     @pl.when(jnp.logical_not(crossed))
     def _():
@@ -183,7 +203,94 @@
         scores_of(2 - hop)
     for s in range(2):
         halo(2, s).wait_recv()
+    def column_slot(step):
+        return lax.rem(yh + 2 * NX - x - step, NX)
+
+    def across(step):
+        return send(
+            s1.at[column_slot(step)], a2.at[step], s2_send.at[step], s2_recv.at[step],
+            (x_tok(step), h),
+        )
+
+    def landed_at(slot):
+        send(
+            hid_in, s1.at[slot], s1_send.at[slot], s1_recv.at[slot], (t_next, h)
+        ).wait_recv()
+
+    def relay(slot, step):
+        after = (slot + step) % NYH
+        return send(
+            s1.at[slot], s1.at[after], relay_send.at[after], s1_recv.at[after],
+            (t, head_at(step)),
+        )
+
+    def move_on(slot):
+        step = lax.rem(yh + 2 * NX - x - slot, NX)
+
+        @pl.when(step > 0)
+        def _():
+            send(
+                s1.at[slot], a2.at[step], s2_send.at[step], s2_recv.at[step], (x_tok(step), h)
+            ).start()
+
+        @pl.when(step == 0)
+        def _():
+            share(0).start()
+
+    def first_blocks(act):
+        @pl.when(case_same_low)
+        def _():
+            act(((1, 1), (3, 0), (0, 0)))
+
+        @pl.when(case_same_high)
+        def _():
+            act(((3, 3), (1, 0), (0, 0)))
+
+        @pl.when(case_high_low)
+        def _():
+            act(((0, 1), (3, 3)))
+
+        @pl.when(case_low_high)
+        def _():
+            act(((1, 1), (0, 3)))
+
+    def take_first(blocks):
+        for slot, step in blocks:
+            landed_at(slot)
+            if step:
+                relay(slot, step).start()
+        for slot, step in blocks:
+            move_on(slot)
+
+    def take_second():
+        def take(slot):
+            landed_at(slot)
+            move_on(slot)
+
+        @pl.when(jnp.logical_not(crossed))
+        def _():
+            take(2)
+
+        @pl.when(case_high_low)
+        def _():
+            take(1)
+            take(2)
+
+        @pl.when(case_low_high)
+        def _():
+            take(2)
+            take(3)
+
+    def own_block(step):
+        return s1.at[column_slot(0)] if step == 0 else a2.at[step]
+
+    def share(step):
+        return send(
+            own_block(step), a3.at[step], s3_send.at[step], s3_recv.at[step], (t, sibling)
+        )
+
     scores_of(0)
+    first_blocks(take_first)
 
     for pair in range(PAIRS):
         top = st_m[0, pair]
@@ -238,36 +345,13 @@
         else:
             bb[s, 0] = mine.astype(BF16)
 
-    def column_slot(step):
-        return lax.rem(yh + 2 * NX - x - step, NX)
-
-    def across(step):
-        return send(
-            s1.at[column_slot(step)], a2.at[step], s2_send.at[step], s2_recv.at[step],
-            (x_tok(step), h),
-        )
-
-    def own_block(step):
-        return s1.at[column_slot(0)] if step == 0 else a2.at[step]
-
-    def share(step):
-        return send(
-            own_block(step), a3.at[step], s3_send.at[step], s3_recv.at[step], (t, sibling)
-        )
-
     grads_of(0)
     hand_over(0, 1)
     hand_over(0, 0)
     grads_of(1)
     hand_over(1, 1)
     hand_over(1, 0)
-    for step in (2, 1, 3, 0):
-        slot = column_slot(step)
-        send(
-            hid_in, s1.at[slot], s1_send.at[slot], s1_recv.at[slot], (t_next, h)
-        ).wait_recv()
-        if step:
-            across(step).start()
+    take_second()
     grads_of(2)
     hand_over(2, 1)
     hand_over(2, 0)
@@ -315,10 +399,16 @@
         own_up(s).start()
         own_down(s).start()
 
-    share(0).start()
+    def slot_of(step, dy):
+        return step * NYL + dy
+
+    near = lax.rem(yl + core, 2)
     for step in range(1, NX):
         across(step).wait_recv()
         share(step).start()
+    at[near] = jnp.transpose(s1[column_slot(0)])
+    for step in range(1, NX):
+        at[slot_of(step, near)] = jnp.transpose(a2[step])
 
     for s in (1, 0):
         from_pair(s).wait_recv()
@@ -327,21 +417,13 @@
         own_up(s).wait_recv()
         own_far(s).start()
 
-    def slot_of(step, dy):
-        return step * NYL + dy
-
-    near = lax.rem(yl + core, 2)
-    at[near] = jnp.transpose(s1[column_slot(0)])
-    for step in range(1, NX):
-        at[slot_of(step, near)] = jnp.transpose(a2[step])
+    for step in range(NX):
+        share(step).wait_recv()
+        at[slot_of(step, 1 - near)] = jnp.transpose(a3[step])
 
     for s in (1, 0):
         pair_down(s).wait_recv()
         pair_far(s).start()
-
-    for step in range(NX):
-        share(step).wait_recv()
-        at[slot_of(step, 1 - near)] = jnp.transpose(a3[step])
 
     def scatter(s, step):
         return send(
@@ -372,13 +454,14 @@
         for s in range(2):
             halo(hop, s).wait_send()
             pass_back(hop, s).wait_send()
-    for step in range(1, NYH):
-        fan(step).wait_send()
-
-    @pl.when(crossed)
-    def _():
-        fan(0).wait_send()
-
+    sends(lambda step: fan(step).wait_send())
+
+    def relays_left(blocks):
+        for slot, step in blocks:
+            if step:
+                relay(slot, step).wait_send()
+
+    first_blocks(relays_left)
     for step in range(NX):
         if step:
             across(step).wait_send()
@@ -439,11 +522,11 @@
             vmem((2, NZ, OUT_ROWS, HD), BF16),
             vmem((2, NZ, OUT_ROWS, HD), BF16),
             dma((6,)), dma((2,)), dma((3, 2)), dma((3, 2)), dma((3, 2)), dma((3, 2)),
-            dma((NYH,)), dma((NYH,)), dma((NX,)), dma((NX,)), dma((NX,)), dma((NX,)),
+            dma((NYH,)), dma((NYH,)), dma((NYH,)), dma((NX,)), dma((NX,)), dma((NX,)), dma((NX,)),
             dma((2, SLOTS)), dma((2, SLOTS)), dma((2, NZ)), dma((2, NZ)),
         ],
         compiler_params=pltpu.CompilerParams(
-            collective_id=0, has_side_effects=True, vmem_limit_bytes=48 << 20
+            collective_id=0, has_side_effects=True, vmem_limit_bytes=67043328
         ),
     )(
         queries_first,

time: 86 us -> 79.1 us (0.920)
  the two profiles are of different devices: /device:TPU:10 before, /device:TPU:56 now
where the time goes in v3:
time: 79.1 us; the launch traced here: 78.9 us
  Pallas kernels  75.2 us (95%)
  local copies, waits for them, and re-layouts  3.01 us (4%)
    pallas_call x1, Pallas kernels, body(): pl.pallas_call(kernel, out_shape=(jax.ShapeDtypeStruct((ROWS, WIDTH), BF1...  75.2 us
    unnamed x7, local copies, waits for them, and re-layouts  3.01 us

profile of v3, /device:TPU:56, one launch (start us, length us, event | category | flops | bytes accessed | tf_op | source)
XLA Modules:
  0.0 78.9 jit_solution(532974770618867981)
XLA Ops:
  0.6 75.2 %shard_map.103 = (bf16[256,384]{1,0:T(8,128)(2,1)}, bf16[256,384]{1,0:T(8,128)(2,1)}, f32[24,256]{1,0:T(8,128)}) custom-call(bf16[256,384]{1,0:T(8,128)(2,1)} %q1_in.1, bf16[256,384]{1,0:T(8,128)(2,1)} %q2_in.1, bf16[256,384]{1,0:T(8,128)(2,1)} %g1_in.1, bf16[256,384]{1,0:T(8,128)(2,1)} %g2_in.1, bf16[256,128]{1,0:T(8,128)(2,1)} %k_in.1, ...), custom_call_target="tpu_custom_call" | custom-call | tf_op jit(solution)/shard_map/pallas_call | solution.py:490
  75.9 0.0 copy-start
  75.9 1.7 %copy.14 = bf16[256,384]{1,0:T(8,128)(2,1)} copy(bf16[256,384]{1,0:T(8,128)(2,1)} %get-tuple-element.6) | data formatting | bytes 393216
  77.5 0.0 copy-done
  77.5 0.0 copy-start.1
  77.5 0.7 copy.15
  78.2 0.1 copy-done.1
  78.3 0.6 copy.16
Async XLA Ops:
  75.9 1.7 %copy-start = (bf16[256,384]{1,0:T(8,128)(2,1)S(1)}, bf16[256,384]{1,0:T(8,128)(2,1)}, u32[]{:S(2)}) copy-start(bf16[256,384]{1,0:T(8,128)(2,1)} %get-tuple-element.7) | copy-start | bytes 589828
  77.5 0.7 copy-start.1
